TPU v7x, 32 devices: a whole 2x2x4 slice. The times are simulated.
32 devices in a mesh: dp: 4 (over y, x), ctx: 8 (over z, core).
Axes of the slice: x: 2, y: 2, z: 4, core: 2. Of those that a mesh axis runs over, the one named last changes fastest.
Arguments:
- query_rows: bfloat16 [4, 1024, 1024], P('dp', 'ctx'), may hold values from -0.59765625 to 0.59765625
- key_rows: bfloat16 [4, 1024, 1024], P('dp', 'ctx'), may hold values from -0.59765625 to 0.59765625
- value_rows: bfloat16 [4, 1024, 2048], P('dp', 'ctx'), may hold values from -6 to 6
- log_decay: bfloat16 [4, 1024, 1024], P('dp', 'ctx'), may hold values from -1 to 0, as said below
- out_grad: bfloat16 [4, 1024, 2048], P('dp', 'ctx'), may hold values from -1.796875 to 1.796875
- doc_ids: int32 [4, 1024], P('dp', 'ctx'), may hold values from 0 to 3, as said below
- block_order: int32 [4, 8, 4], P(None, 'ctx'), may hold values from 0 to 3, each once within a row
Outputs:
- attn_out: bfloat16 [4, 1024, 2048], P('dp', 'ctx')
- query_grad: bfloat16 [4, 1024, 1024], P('dp', 'ctx')
- key_grad: bfloat16 [4, 1024, 1024], P('dp', 'ctx')
- value_grad: bfloat16 [4, 1024, 2048], P('dp', 'ctx')
- decay_grad: bfloat16 [4, 1024, 1024], P('dp', 'ctx')
Inputs may be any that keep to these rules, and one draw needn't show every extreme that they name: `log_decay`: nonpositive. `doc_ids`: never falls along a pack; every document number of a pack is used; each document has 1 to 512 positions, one of them exactly 512 and one 8 or fewer. `block_order`: each row of a device's list names each of its 4 blocks once.
All inputs are finite; a program needn't handle non-finite values.
Results may differ from a plain program's by a relative error of at most 0.0015.
Values may be sent and summed in bfloat16 or wider, within the bound.
A program may use at most 192 MiB of HBM per device.

v0:
```python
import jax
import jax.numpy as jnp
from jax import lax
from jax.sharding import PartitionSpec as P

DK = 64
DV = 128
BLK = 32
HIGH = lax.Precision.HIGHEST


def prefix(part, axis, combine, identity, reverse):
    count = lax.axis_size(axis)
    place = lax.axis_index(axis)
    ahead = count - 1 - place if reverse else place
    gathered = jax.tree.map(lambda a: lax.all_gather(a, axis), part)
    state = jax.tree.map(lambda a, e: jnp.zeros_like(a) + jnp.asarray(e, a.dtype), part, identity)

    def one(hop, state):
        source = count - 1 - hop if reverse else hop
        return combine(
            state, jax.tree.map(lambda a: lax.dynamic_index_in_dim(a, source, 0, False), gathered)
        )

    return lax.fori_loop(0, ahead, one, state)


def prepare(query_b, key_b, value_b, decay_b, doc_row):
    row_count = query_b.shape[0]
    head_count = query_b.shape[1] // DK
    query_f = query_b.astype(jnp.float32).reshape(row_count, head_count, DK)
    key_f = key_b.astype(jnp.float32).reshape(row_count, head_count, DK)
    value_f = value_b.astype(jnp.float32).reshape(row_count, head_count, DV)
    cumul = jnp.cumsum(decay_b.astype(jnp.float32).reshape(row_count, head_count, DK), axis=0)
    total_log = cumul[-1]
    growth = jnp.exp(cumul)
    shrink = jnp.exp(-cumul)
    to_end = jnp.exp(total_log[None] - cumul)
    later_pos = lax.broadcasted_iota(jnp.int32, (row_count, row_count), 0)
    earlier_pos = lax.broadcasted_iota(jnp.int32, (row_count, row_count), 1)
    same_doc = ((later_pos >= earlier_pos) & (doc_row[:, None] == doc_row[None, :])).astype(
        jnp.float32
    )
    first_id = doc_row[0]
    last_id = doc_row[-1]
    in_first = (doc_row == first_id).astype(jnp.float32)[:, None, None]
    in_last = (doc_row == last_id).astype(jnp.float32)[:, None, None]
    query_t = query_f * growth
    key_t = key_f * shrink
    scores = jnp.einsum("thi,shi->hts", query_t, key_t, precision=HIGH) * same_doc[None]
    return {
        "query_f": query_f,
        "key_f": key_f,
        "value_f": value_f,
        "growth": growth,
        "shrink": shrink,
        "to_end": to_end,
        "same_doc": same_doc,
        "first_id": first_id,
        "last_id": last_id,
        "in_first": in_first,
        "in_last": in_last,
        "query_t": query_t,
        "key_t": key_t,
        "scores": scores,
        "decay_all": jnp.exp(total_log),
    }


def state_end(parts):
    return jnp.einsum(
        "shi,shj->hij",
        parts["key_f"] * parts["to_end"] * parts["in_last"],
        parts["value_f"],
        precision=HIGH,
    )


def start_grad(parts, grad_f):
    factor = DK ** (-0.5)
    return factor * jnp.einsum(
        "thi,thj->hij", parts["query_t"] * parts["in_first"], grad_f, precision=HIGH
    )


def finish(parts, grad_f, state_in, use_state, carry_in, use_carry):
    factor = DK ** (-0.5)
    head_w = parts["in_first"] * use_state
    tail_w = parts["in_last"] * use_carry
    attn_rows = factor * (
        jnp.einsum("hts,shj->thj", parts["scores"], parts["value_f"], precision=HIGH)
        + jnp.einsum("thi,hij->thj", parts["query_t"], state_in, precision=HIGH) * head_w
    )
    grad_scores = (
        jnp.einsum("thj,shj->hts", grad_f, parts["value_f"], precision=HIGH)
        * parts["same_doc"][None]
    )
    grad_query = (
        factor
        * parts["growth"]
        * (
            jnp.einsum("hts,shi->thi", grad_scores, parts["key_t"], precision=HIGH)
            + jnp.einsum("thj,hij->thi", grad_f, state_in, precision=HIGH) * head_w
        )
    )
    grad_value = (
        factor * jnp.einsum("hts,thj->shj", parts["scores"], grad_f, precision=HIGH)
        + jnp.einsum("shi,hij->shj", parts["key_f"] * parts["to_end"], carry_in, precision=HIGH)
        * tail_w
    )
    grad_key = (
        factor
        * parts["shrink"]
        * jnp.einsum("hts,thi->shi", grad_scores, parts["query_t"], precision=HIGH)
        + parts["to_end"]
        * jnp.einsum("hij,shj->shi", carry_in, parts["value_f"], precision=HIGH)
        * tail_w
    )
    grad_log = parts["query_f"] * grad_query - parts["key_f"] * grad_key
    sum_start = jnp.sum(grad_log * parts["in_first"], axis=0)
    return (attn_rows, grad_query, grad_key, grad_value, grad_log, sum_start)


def decay_grad_of(parts, grad_log, sums_in, use_carry):
    inside = jnp.einsum("ts,thi->shi", parts["same_doc"], grad_log, precision=HIGH)
    return inside + sums_in[None] * parts["in_last"] * use_carry


def select_tree(flag, yes_tree, no_tree):
    return tuple((jnp.where(flag, left, right) for left, right in zip(yes_tree, no_tree)))


def join_forward(before, follow):
    b_dec, b_state, b_first, b_last = before
    f_dec, f_state, f_first, f_last = follow
    joined = ((f_first == f_last) & (b_last == f_first)).astype(jnp.float32)
    merged = (
        f_dec * (joined * b_dec + 1.0 - joined),
        f_state + joined * f_dec[..., None] * b_state,
        b_first,
        f_last,
    )
    return select_tree(b_first < 0, follow, select_tree(f_first < 0, before, merged))


def join_backward(before, follow):
    b_dec, b_state, b_first, b_last = before
    f_dec, f_state, f_first, f_last = follow
    joined = ((f_first == f_last) & (f_last == b_first)).astype(jnp.float32)
    merged = (
        f_dec * (joined * b_dec + 1.0 - joined),
        f_state + joined * f_dec[..., None] * b_state,
        f_first,
        b_last,
    )
    return select_tree(b_first < 0, follow, select_tree(f_first < 0, before, merged))


def join_sums(before, follow):
    b_sum, b_first, b_last = before
    f_sum, f_first, f_last = follow
    joined = ((f_first == f_last) & (f_last == b_first)).astype(jnp.float32)
    merged = (f_sum + joined * b_sum, f_first, b_last)
    return select_tree(b_first < 0, follow, select_tree(f_first < 0, before, merged))


def inverse_of(order_lists):
    block_count = order_lists.shape[-1]
    slot_ids = jnp.arange(block_count, dtype=jnp.int32)
    matches = order_lists[..., :, None] == slot_ids
    return jnp.sum(jnp.where(matches, slot_ids[:, None], 0), axis=-2)


def body(query_rows, key_rows, value_rows, log_decay, out_grad, doc_ids, block_order):
    dp_count = lax.axis_size("dp")
    dp_index = lax.axis_index("dp")
    row_count = query_rows.shape[1]
    block_count = row_count // BLK
    per_peer = block_count // dp_count
    order_lists = block_order[:, 0, :]
    my_order = order_lists[dp_index]
    gathered = (
        lax.all_gather(query_rows, "dp", axis=0, tiled=True),
        lax.all_gather(key_rows, "dp", axis=0, tiled=True),
        lax.all_gather(value_rows, "dp", axis=0, tiled=True),
        lax.all_gather(log_decay, "dp", axis=0, tiled=True),
    )
    inverse = inverse_of(order_lists)
    wanted = dp_index * per_peer + jnp.arange(per_peer, dtype=jnp.int32)
    slot_ids = inverse[:, wanted]
    source_ids = jnp.arange(dp_count, dtype=jnp.int32)[:, None]
    balanced = tuple(
        (
            whole.reshape(dp_count, block_count, BLK, whole.shape[-1])[
                source_ids, slot_ids
            ].reshape(row_count, whole.shape[-1])
            for whole in gathered
        )
    )
    query_bal, key_bal, value_bal, decay_bal = balanced
    doc_row = doc_ids[0]
    parts = prepare(query_bal, key_bal, value_bal, decay_bal, doc_row)
    head_count = parts["query_f"].shape[1]
    grad_f = out_grad[0].astype(jnp.float32).reshape(row_count, head_count, DV)
    first_f = parts["first_id"].astype(jnp.float32)
    last_f = parts["last_id"].astype(jnp.float32)
    neutral = (
        jnp.ones((head_count, DK), jnp.float32),
        jnp.zeros((head_count, DK, DV), jnp.float32),
        jnp.float32(-1.0),
        jnp.float32(-1.0),
    )
    unused_dec, state_in, unused_first, prior_last = prefix(
        (parts["decay_all"], state_end(parts), first_f, last_f), "ctx", join_forward, neutral, False
    )
    use_state = (prior_last == first_f).astype(jnp.float32)
    other_dec, carry_in, next_first, other_last = prefix(
        (parts["decay_all"], start_grad(parts, grad_f), first_f, last_f),
        "ctx",
        join_backward,
        neutral,
        True,
    )
    use_carry = (next_first == last_f).astype(jnp.float32)
    attn_rows, grad_query, grad_key, grad_value, grad_log, sum_start = finish(
        parts, grad_f, state_in, use_state, carry_in, use_carry
    )
    sums_in, later_first, later_last = prefix(
        (sum_start, first_f, last_f),
        "ctx",
        join_sums,
        (jnp.zeros((head_count, DK), jnp.float32), jnp.float32(-1.0), jnp.float32(-1.0)),
        True,
    )
    use_sums = (later_first == last_f).astype(jnp.float32)
    grad_decay = decay_grad_of(parts, grad_log, sums_in, use_sums)
    attn_out = attn_rows.reshape(row_count, head_count * DV).astype(jnp.bfloat16)[None]
    query_back = grad_query.reshape(row_count, head_count * DK).astype(jnp.bfloat16)
    key_back = grad_key.reshape(row_count, head_count * DK).astype(jnp.bfloat16)
    value_back = grad_value.reshape(row_count, head_count * DV).astype(jnp.bfloat16)
    decay_back = grad_decay.reshape(row_count, head_count * DK).astype(jnp.bfloat16)
    gathered_back = (
        lax.all_gather(query_back[None], "dp", axis=0, tiled=True),
        lax.all_gather(key_back[None], "dp", axis=0, tiled=True),
        lax.all_gather(value_back[None], "dp", axis=0, tiled=True),
        lax.all_gather(decay_back[None], "dp", axis=0, tiled=True),
    )
    dest_ids = my_order // per_peer
    dest_slots = dp_index * per_peer + my_order % per_peer
    returned = tuple(
        (
            whole.reshape(dp_count, block_count, BLK, whole.shape[-1])[
                dest_ids, dest_slots
            ].reshape(1, row_count, whole.shape[-1])
            for whole in gathered_back
        )
    )
    query_grad, key_grad, value_grad, decay_grad = returned
    return (attn_out, query_grad, key_grad, value_grad, decay_grad)


def solution(mesh):
    placed = (
        P("dp", "ctx", None),
        P("dp", "ctx", None),
        P("dp", "ctx", None),
        P("dp", "ctx", None),
        P("dp", "ctx", None),
        P("dp", "ctx"),
        P(None, "ctx", None),
    )
    return jax.shard_map(
        body,
        mesh=mesh,
        in_specs=placed,
        out_specs=(
            P("dp", "ctx", None),
            P("dp", "ctx", None),
            P("dp", "ctx", None),
            P("dp", "ctx", None),
            P("dp", "ctx", None),
        ),
        check_vma=False,
    )
```

profile of v0, /device:TPU:0, one launch (start us, length us, event | category | flops | bytes accessed | tf_op | source)
XLA Modules:
  0.0 467.1 jit_solution(8892131721895761153)
XLA Ops:
  12.3 1.3 fusion.43
  13.6 1.8 compare_convert_fusion
  15.5 23.7 %all-gather.18.cloned.1.call-done = bf16[4,128,1024]{2,1,0:T(8,128)(2,1)} async-done(((bf16[1,128,1024]{2,1,0:T(8,128)(2,1)}), bf16[4,128,1024]{2,1,0:T(8,128)(2,1)}) %all-gather.18.cloned.1.call-update) | async-done | bytes 1048592 | tf_op jit(solution)/shard_map/all_gather | solution.py:186
  39.2 1.8 gather_fusion.2
  41.0 1.3 reshape.327
  42.3 1.4 fusion.44
  44.1 23.6 %all-gather.16.cloned.1.call-done = bf16[4,128,1024]{2,1,0:T(8,128)(2,1)} async-done(((bf16[1,128,1024]{2,1,0:T(8,128)(2,1)}), bf16[4,128,1024]{2,1,0:T(8,128)(2,1)}) %all-gather.16.cloned.1.call-update) | async-done | bytes 1048592 | tf_op jit(solution)/shard_map/all_gather | solution.py:183
  67.7 1.8 gather_fusion.1
  70.8 1.6 copy.125
  72.5 1.9 convolution_multiply_fusion.4
  74.6 21.7 %all-gather.20.cloned.1.call-done = bf16[4,128,1024]{2,1,0:T(8,128)(2,1)} async-done(((bf16[1,128,1024]{2,1,0:T(8,128)(2,1)}), bf16[4,128,1024]{2,1,0:T(8,128)(2,1)}) %all-gather.20.cloned.1.call-update) | async-done | bytes 1048592 | tf_op jit(solution)/shard_map/all_gather | solution.py:184
  96.2 1.8 gather_fusion.3
  99.3 1.6 copy.127
  101.6 31.6 %all-gather.14.cloned.1.call-done = bf16[4,128,2048]{2,1,0:T(8,128)(2,1)} async-done(((bf16[1,128,2048]{2,1,0:T(8,128)(2,1)}), bf16[4,128,2048]{2,1,0:T(8,128)(2,1)}) %all-gather.14.cloned.1.call-update) | async-done | bytes 2097168 | tf_op jit(solution)/shard_map/all_gather | solution.py:185
  133.3 2.2 gather_fusion
  135.6 1.5 fusion.18
  140.4 17.0 %all-reduce.3 = (f32[8]{0:T(128)S(1)}, f32[8]{0:T(128)S(1)}) all-reduce(f32[8]{0:T(128)S(1)} %dynamic-update-slice.1, f32[8]{0:T(128)S(1)} %dynamic-update-slice.2), channel_id=1, replica_groups=mesh['dp'=4,'ctx'=8] {'ctx'}, use_global_device_ids=true, to_apply=%add.1 | all-reduce | flops 16 | bytes 128
  157.5 14.2 %all_gather.78 = f32[8,16,64]{2,1,0:T(8,128)S(1)} all-gather(f32[1,16,64]{2,1,0:T(8,128)S(1)} %get-tuple-element.421), channel_id=1, replica_groups=mesh['dp'=4,'ctx'=8] {'ctx'}, dimensions={0}, use_global_device_ids=true | all-gather | bytes 36864 | tf_op jit(solution)/shard_map/all_gather | solution.py:16
  171.7 1.6 fusion.6
  173.2 9.4 %all-gather.32.cloned.1.call-done = f32[128,64,128]{2,1,0:T(8,128)} async-done(((f32[16,64,128]{2,1,0:T(8,128)}), f32[128,64,128]{2,1,0:T(8,128)}) %all-gather.32.cloned.1.call-update) | async-done | bytes 4194320 | tf_op jit(solution)/shard_map/all_gather | solution.py:16
  182.6 45.4 %while.51 = (s32[]{:T(128)}, f32[16,64,128]{2,1,0:T(8,128)S(1)}, f32[]{:T(128)}, s32[]{:T(128)}, f32[8,16,64,128]{3,2,1,0:T(8,128)}, /*index=5*/f32[8]{0:T(128)S...) while((s32[]{:T(128)}, f32[16,64,128]{2,1,0:T(8,128)S(1)}, ...), condition=%wide.region_5.6_spmd, body=%wide.region_4.5_spmd.sunk | while | flops 525326 | bytes 1585431 | solution.py:25
  186.4 1.5 bitcast_select_fusion.7
  192.9 1.5 bitcast_select_fusion.7
  199.3 1.5 bitcast_select_fusion.7
  205.8 1.5 bitcast_select_fusion.7
  212.3 1.5 bitcast_select_fusion.7
  218.8 1.5 bitcast_select_fusion.7
  225.3 1.5 bitcast_select_fusion.7
  228.0 2.5 all-gather.30.cloned.1.call-done
  230.6 1.3 compare_select_fusion.3
  233.7 2.2 fusion.12
  235.9 2.1 multiply_reduce_fusion
  239.2 61.9 %all-gather.2 = f32[128,64]{1,0:T(8,128)S(1)} all-gather(f32[16,64]{1,0:T(8,128)S(1)} %get-tuple-element.419), channel_id=4, replica_groups=mesh['dp'=4,'ctx'=8] {'ctx'}, dimensions={0}, use_global_device_ids=true | all-gather | bytes 36864 | tf_op jit(solution)/shard_map/all_gather | solution.py:16
  301.0 34.3 %while.52 = (s32[]{:T(128)}, f32[16,64]{1,0:T(8,128)S(1)}, f32[]{:T(128)}, s32[]{:T(128)}, f32[8,16,64]{2,1,0:T(8,128)S(1)}, /*index=5*/f32[8]{0:T(128)S(1)}, f3...) while((s32[]{:T(128)}, f32[16,64]{1,0:T(8,128)S(1)}, f32[]{:T(128)}, ...), condition=%wide.region_8.9_spmd, body=%wide.region_7.8_spmd.sunk | while | flops 4110 | bytes 12555 | solution.py:25
  337.5 1.8 copy.139
  339.4 1.8 copy.136
  341.2 2.9 convolution_multiply_fusion.3
  346.1 2.8 fusion.9
  352.0 2.4 fusion.24
  354.4 1.8 fusion.10
  357.3 5.4 %all-gather.28.cloned.1.call-done = bf16[4,128,1024]{2,1,0:T(8,128)(2,1)} async-done(((bf16[1,128,1024]{2,1,0:T(8,128)(2,1)}), bf16[4,128,1024]{2,1,0:T(8,128)(2,1)}) %all-gather.28.cloned.1.call-update) | async-done | bytes 1048592 | tf_op jit(solution)/shard_map/all_gather | solution.py:246
  362.6 2.5 gather_fusion.7
  365.1 26.0 %all-gather.24.cloned.1.call-done = bf16[4,128,1024]{2,1,0:T(8,128)(2,1)} async-done(((bf16[1,128,1024]{2,1,0:T(8,128)(2,1)}), bf16[4,128,1024]{2,1,0:T(8,128)(2,1)}) %all-gather.24.cloned.1.call-update) | async-done | bytes 1048592 | tf_op jit(solution)/shard_map/all_gather | solution.py:244
  391.1 2.5 gather_fusion.5
  393.6 26.6 %all-gather.22.cloned.1.call-done = bf16[4,128,1024]{2,1,0:T(8,128)(2,1)} async-done(((bf16[1,128,1024]{2,1,0:T(8,128)(2,1)}), bf16[4,128,1024]{2,1,0:T(8,128)(2,1)}) %all-gather.22.cloned.1.call-update) | async-done | bytes 1048592 | tf_op jit(solution)/shard_map/all_gather | solution.py:243
  420.2 2.5 gather_fusion.4
  422.7 34.5 %all-gather.26.cloned.1.call-done = bf16[4,128,2048]{2,1,0:T(8,128)(2,1)} async-done(((bf16[1,128,2048]{2,1,0:T(8,128)(2,1)}), bf16[4,128,2048]{2,1,0:T(8,128)(2,1)}) %all-gather.26.cloned.1.call-update) | async-done | bytes 2097168 | tf_op jit(solution)/shard_map/all_gather | solution.py:245
  457.3 3.0 gather_fusion.6
  (115 shorter events, 39.7 us)
Async XLA Ops:
  7.2 32.0 %all-gather.18.cloned.1.call-start = ((), (), s32[]{:S(2)}) async-start(), calls=%async_computation.2 | async-start | bytes 1310720 | tf_op jit(solution)/shard_map/all_gather | solution.py:186
  7.9 59.8 %all-gather.16.cloned.1.call-start = ((), (), s32[]{:S(2)}) async-start(), calls=%async_computation.1 | async-start | bytes 1310720 | tf_op jit(solution)/shard_map/all_gather | solution.py:183
  8.6 87.6 %all-gather.20.cloned.1.call-start = ((), (), s32[]{:S(2)}) async-start(), calls=%async_computation.3 | async-start | bytes 1310720 | tf_op jit(solution)/shard_map/all_gather | solution.py:184
  9.4 123.9 %all-gather.14.cloned.1.call-start = ((), (), s32[]{:S(2)}) async-start(), calls=%async_computation | async-start | bytes 2621440 | tf_op jit(solution)/shard_map/all_gather | solution.py:185
  10.0 172.6 %all-gather.32.cloned.1.call-start = ((), (), s32[]{:S(2)}) async-start(), calls=%async_computation.9 | async-start | bytes 4718592 | tf_op jit(solution)/shard_map/all_gather | solution.py:16
  43.7 25.8 %copy-start.7 = (f32[128,16,64]{2,1,0:T(8,128)}, f32[128,16,64]{2,1,0:T(8,128)S(1)}, u32[]{:S(2)}) copy-start(f32[128,16,64]{2,1,0:T(8,128)S(1)} %fusion.44) | copy-start | bytes 1572868
  72.4 25.6 %copy-start.5 = (f32[128,16,64]{0,2,1:T(8,128)}, f32[128,16,64]{0,2,1:T(8,128)S(1)}, u32[]{:S(2)}) copy-start(f32[128,16,64]{0,2,1:T(8,128)S(1)} %copy.125) | copy-start | bytes 1572868
  72.5 62.9 %copy-start = (f32[128,16,64]{0,2,1:T(8,128)}, f32[128,16,64]{0,2,1:T(8,128)S(1)}, u32[]{:S(2)}) copy-start(f32[128,16,64]{0,2,1:T(8,128)S(1)} %exponential_multiply_fusion) | copy-start | bytes 1572868
  74.5 63.8 %copy-start.9 = (u32[32]{0:T(128)S(1)}, u32[32]{0:T(128)}, u32[]{:S(2)}) copy-start(u32[32]{0:T(128)} %constant.302) | copy-start | bytes 388
  74.5 82.9 %copy-start.8 = (s32[1,128]{1,0:T(1,128)S(1)}, s32[1,128]{1,0:T(1,128)}, u32[]{:S(2)}) copy-start(s32[1,128]{1,0:T(1,128)} %param.18) | copy-start | bytes 1540
  74.5 156.0 %all-gather.30.cloned.1.call-start = ((), (), s32[]{:S(2)}) async-start(), calls=%async_computation.8 | async-start | bytes 4718592 | tf_op jit(solution)/shard_map/all_gather | solution.py:16
  137.1 225.6 %all-gather.28.cloned.1.call-start = ((), (), s32[]{:S(2)}) async-start(), calls=%async_computation.7 | async-start | bytes 1310720 | tf_op jit(solution)/shard_map/all_gather | solution.py:246
  230.6 3.1 copy-start.3
  230.6 5.2 %copy-start.1 = (f32[128,16,64]{0,2,1:T(8,128)S(1)}, f32[128,16,64]{0,2,1:T(8,128)}, u32[]{:S(2)}) copy-start(f32[128,16,64]{0,2,1:T(8,128)} %copy-done) | copy-start | bytes 1572868
  230.6 5.2 %copy-start.6 = (f32[128,16,64]{0,2,1:T(8,128)S(1)}, f32[128,16,64]{0,2,1:T(8,128)}, u32[]{:S(2)}) copy-start(f32[128,16,64]{0,2,1:T(8,128)} %copy-done.5) | copy-start | bytes 1572868
  337.4 53.7 %all-gather.24.cloned.1.call-start = ((), (), s32[]{:S(2)}) async-start(), calls=%async_computation.5 | async-start | bytes 1310720 | tf_op jit(solution)/shard_map/all_gather | solution.py:244
  339.3 80.9 %all-gather.22.cloned.1.call-start = ((), (), s32[]{:S(2)}) async-start(), calls=%async_computation.4 | async-start | bytes 1310720 | tf_op jit(solution)/shard_map/all_gather | solution.py:243
  341.2 116.1 %all-gather.26.cloned.1.call-start = ((), (), s32[]{:S(2)}) async-start(), calls=%async_computation.6 | async-start | bytes 2621440 | tf_op jit(solution)/shard_map/all_gather | solution.py:245
  344.1 1.0 copy-start.4
  346.1 8.3 %copy-start.2 = (f32[128,16,64]{0,2,1:T(8,128)S(1)}, f32[128,16,64]{0,2,1:T(8,128)}, u32[]{:S(2)}) copy-start(f32[128,16,64]{0,2,1:T(8,128)} %copy-done) | copy-start | bytes 1572868
Sparse Core Ops, SparseCore 0:
  9.8 29.3 all-gather.17
  41.0 26.6 all-gather.15
  69.6 26.6 all-gather.19
  97.9 35.2 all-gather.13
  134.7 47.8 all-gather.31
  184.6 45.8 all-gather.29
  337.6 25.0 all-gather.27
  364.5 26.6 all-gather.23
  393.6 26.6 all-gather.21
  421.9 35.2 all-gather.25
where the time goes:
time: 469 us; the launch traced here: 467 us
  waiting for transfers between devices  208 us (44%)
  blocking collectives  93 us (20%)
  local copies, waits for them, and re-layouts  57.1 us (12%)
  loops' own time  52.2 us (11%)
  matrix products  23.1 us (5%)
  other arithmetic  18 us (4%)
  between operations  15.7 us (3%)
    all_gather x2, blocking collectives, prefix(): gathered = jax.tree.map(lambda a: lax.all_gather(a, axis), part)  76 us
    another operation x3, loops' own time, prefix(): return lax.fori_loop(0, ahead, one, state)  52.2 us
    all_gather x1, waiting for transfers between devices, body(): lax.all_gather(value_back[None], 'dp', axis=0, tiled=True)  34.5 us
    all_gather x1, waiting for transfers between devices, body(): lax.all_gather(value_rows, 'dp', axis=0, tiled=True)  31.6 us
    all_gather x1, waiting for transfers between devices, body(): lax.all_gather(query_back[None], 'dp', axis=0, tiled=True)  26.6 us
    all_gather x1, waiting for transfers between devices, body(): lax.all_gather(key_back[None], 'dp', axis=0, tiled=True)  26 us
    all_gather x1, waiting for transfers between devices, body(): lax.all_gather(log_decay, 'dp', axis=0, tiled=True)  23.7 us
    all_gather x1, waiting for transfers between devices, body(): lax.all_gather(query_rows, 'dp', axis=0, tiled=True)  23.6 us
  transfers between devices with their start and end apart: 10, of which 10 were waited for; matrix products, arithmetic and copies ran while one was open for 16% of the time, Pallas kernels for 0%

commit v1 on v0

--- a/solution.py
+++ b/solution.py
@@ -7,6 +7,16 @@
 DV = 128
 BLK = 32
 HIGH = lax.Precision.HIGHEST
+
+
+def gather_around(x, axis, dim):
+    ways, here, step = (lax.axis_size(axis), lax.axis_index(axis), x.shape[dim])
+    dims = [n * ways if d == dim else n for d, n in enumerate(x.shape)]
+    full = lax.dynamic_update_slice_in_dim(jnp.zeros(dims, x.dtype), x, here * step, axis=dim)
+    for far in range(1, ways):
+        x = lax.ppermute(x, axis, [(d, (d + 1) % ways) for d in range(ways)])
+        full = lax.dynamic_update_slice_in_dim(full, x, (here - far) % ways * step, axis=dim)
+    return full
 
 
 def prefix(part, axis, combine, identity, reverse):
@@ -180,7 +190,7 @@
     order_lists = block_order[:, 0, :]
     my_order = order_lists[dp_index]
     gathered = (
-        lax.all_gather(query_rows, "dp", axis=0, tiled=True),
+        gather_around(query_rows, "dp", 0),
         lax.all_gather(key_rows, "dp", axis=0, tiled=True),
         lax.all_gather(value_rows, "dp", axis=0, tiled=True),
         lax.all_gather(log_decay, "dp", axis=0, tiled=True),

time: 469 us -> 448 us (0.955)
  waiting for transfers between devices: 208 us -> 182 us
    ppermute x0 -> x3, waiting for transfers between devices: none -> 24 us  [gather_around(): x = lax.ppermute(x, axis, [(d, (d + 1) % ways) for d in range(ways)])]
    all_gather x1 -> x0, waiting for transfers between devices: 23.6 us -> none  [body(): lax.all_gather(query_rows, 'dp', axis=0, tiled=True)]
    all_gather x1, waiting for transfers between devices: 23.7 us -> 0.18 us  [body(): lax.all_gather(log_decay, 'dp', axis=0, tiled=True)]
  transfers between devices with their start and end apart: 10 -> 12, of which waited for: 10 -> 12; matrix products, arithmetic and copies ran while one was open for 16% -> 16% of each run, Pallas kernels for 0% -> 0%
where the time goes in v1:
time: 448 us; the launch traced here: 446 us
  waiting for transfers between devices  182 us (41%)
  blocking collectives  94.3 us (21%)
  local copies, waits for them, and re-layouts  55.3 us (12%)
  loops' own time  53.9 us (12%)
  matrix products  23.1 us (5%)
  other arithmetic  18 us (4%)
  between operations  15.6 us (3%)
    all_gather x2, blocking collectives, prefix(): gathered = jax.tree.map(lambda a: lax.all_gather(a, axis), part)  77.3 us
    another operation x3, loops' own time, prefix(): return lax.fori_loop(0, ahead, one, state)  53.9 us
    all_gather x1, waiting for transfers between devices, body(): lax.all_gather(value_back[None], 'dp', axis=0, tiled=True)  34.7 us
    all_gather x1, waiting for transfers between devices, body(): lax.all_gather(value_rows, 'dp', axis=0, tiled=True)  32.5 us
    all_gather x1, waiting for transfers between devices, body(): lax.all_gather(query_back[None], 'dp', axis=0, tiled=True)  26.6 us
    all_gather x1, waiting for transfers between devices, body(): lax.all_gather(key_back[None], 'dp', axis=0, tiled=True)  26 us
    ppermute x3, waiting for transfers between devices, gather_around(): x = lax.ppermute(x, axis, [(d, (d + 1) % ways) for d in range(ways)])  24 us
    all_gather x1, waiting for transfers between devices, body(): lax.all_gather(key_rows, 'dp', axis=0, tiled=True)  20.7 us
  transfers between devices with their start and end apart: 12, of which 12 were waited for; matrix products, arithmetic and copies ran while one was open for 16% of the time, Pallas kernels for 0%

profile of v1, /device:TPU:0, one launch (start us, length us, event | category | flops | bytes accessed | tf_op | source)
XLA Modules:
  0.0 446.4 jit_solution(9191120910428763536)
XLA Ops:
  9.4 3.0 collective-permute-start
  13.4 6.5 %collective-permute-done = bf16[1,128,1024]{2,1,0:T(8,128)(2,1)S(1)} collective-permute-done((bf16[1,128,1024]{2,1,0:T(8,128)(2,1)}, bf16[1,128,1024]{2,1,0:T(8,128)(2,1)S(1)}, u32[]{:S(2)}, u32[]{:S(2)}) %collective-permute-start) | collective-permute-done | bytes 262176 | tf_op jit(solution)/shard_map/ppermute | solution.py:17
  20.7 1.3 fusion.40
  22.0 1.9 compare_convert_fusion
  23.9 7.2 %collective-permute-done.1 = bf16[1,128,1024]{2,1,0:T(8,128)(2,1)S(1)} collective-permute-done((bf16[1,128,1024]{2,1,0:T(8,128)(2,1)S(1)}, bf16[1,128,1024]{2,1,0:T(8,128)(2,1)S(1)}, u32[]{:S(2)}, u32[]{:S(2)}) %collective-permute-start.1) | collective-permute-done | bytes 262176 | tf_op jit(solution)/shard_map/ppermute | solution.py:17
  32.3 1.3 copy.152
  33.7 10.3 %collective-permute-done.2 = bf16[1,128,1024]{2,1,0:T(8,128)(2,1)S(1)} collective-permute-done((bf16[1,128,1024]{2,1,0:T(8,128)(2,1)S(1)}, bf16[1,128,1024]{2,1,0:T(8,128)(2,1)S(1)}, u32[]{:S(2)}, u32[]{:S(2)}) %collective-permute-start.2) | collective-permute-done | bytes 262176 | tf_op jit(solution)/shard_map/ppermute | solution.py:17
  45.5 1.8 gather_fusion.2
  48.6 1.4 fusion.41
  51.2 1.9 convolution_multiply_fusion.4
  53.3 20.7 %all-gather.17.cloned.1.call-done = bf16[4,128,1024]{2,1,0:T(8,128)(2,1)} async-done(((bf16[1,128,1024]{2,1,0:T(8,128)(2,1)}), bf16[4,128,1024]{2,1,0:T(8,128)(2,1)}) %all-gather.17.cloned.1.call-update) | async-done | bytes 1048592 | tf_op jit(solution)/shard_map/all_gather | solution.py:194
  74.0 1.8 gather_fusion.3
  77.1 1.6 copy.127
  78.7 32.5 %all-gather.13.cloned.1.call-done = bf16[4,128,2048]{2,1,0:T(8,128)(2,1)} async-done(((bf16[1,128,2048]{2,1,0:T(8,128)(2,1)}), bf16[4,128,2048]{2,1,0:T(8,128)(2,1)}) %all-gather.13.cloned.1.call-update) | async-done | bytes 2097168 | tf_op jit(solution)/shard_map/all_gather | solution.py:195
  111.2 2.2 gather_fusion
  113.5 1.5 fusion.18
  118.4 17.0 %all-reduce.3 = (f32[8]{0:T(128)S(1)}, f32[8]{0:T(128)S(1)}) all-reduce(f32[8]{0:T(128)S(1)} %dynamic-update-slice.1, f32[8]{0:T(128)S(1)} %dynamic-update-slice.2), channel_id=1, replica_groups=mesh['dp'=4,'ctx'=8] {'ctx'}, use_global_device_ids=true, to_apply=%add.1 | all-reduce | flops 16 | bytes 128
  135.5 14.2 %all_gather.74 = f32[8,16,64]{2,1,0:T(8,128)S(1)} all-gather(f32[1,16,64]{2,1,0:T(8,128)S(1)} %get-tuple-element.421), channel_id=1, replica_groups=mesh['dp'=4,'ctx'=8] {'ctx'}, dimensions={0}, use_global_device_ids=true | all-gather | bytes 36864 | tf_op jit(solution)/shard_map/all_gather | solution.py:26
  149.6 1.5 fusion.6
  151.2 9.4 %all-gather.29.cloned.1.call-done = f32[128,64,128]{2,1,0:T(8,128)} async-done(((f32[16,64,128]{2,1,0:T(8,128)}), f32[128,64,128]{2,1,0:T(8,128)}) %all-gather.29.cloned.1.call-update) | async-done | bytes 4194320 | tf_op jit(solution)/shard_map/all_gather | solution.py:26
  160.6 47.0 %while.51 = (s32[]{:T(128)}, f32[16,64,128]{2,1,0:T(8,128)S(1)}, f32[]{:T(128)}, s32[]{:T(128)}, f32[8,16,64,128]{3,2,1,0:T(8,128)}, /*index=5*/f32[8]{0:T(128)S...) while((s32[]{:T(128)}, f32[16,64,128]{2,1,0:T(8,128)S(1)}, ...), condition=%wide.region_5.6_spmd, body=%wide.region_4.5_spmd.sunk | while | flops 525326 | bytes 1585431 | solution.py:35
  164.5 1.5 bitcast_select_fusion.7
  171.2 1.5 bitcast_select_fusion.7
  177.9 1.5 bitcast_select_fusion.7
  184.6 1.5 bitcast_select_fusion.7
  191.3 1.5 bitcast_select_fusion.7
  198.0 1.5 bitcast_select_fusion.7
  204.7 1.5 bitcast_select_fusion.7
  208.8 1.4 compare_select_fusion.3
  211.8 2.2 fusion.12
  214.0 2.1 multiply_reduce_fusion
  217.4 63.1 %all-gather.2 = f32[128,64]{1,0:T(8,128)S(1)} all-gather(f32[16,64]{1,0:T(8,128)S(1)} %get-tuple-element.419), channel_id=4, replica_groups=mesh['dp'=4,'ctx'=8] {'ctx'}, dimensions={0}, use_global_device_ids=true | all-gather | bytes 36864 | tf_op jit(solution)/shard_map/all_gather | solution.py:26
  280.5 34.5 %while.52 = (s32[]{:T(128)}, f32[16,64]{1,0:T(8,128)S(1)}, f32[]{:T(128)}, s32[]{:T(128)}, f32[8,16,64]{2,1,0:T(8,128)S(1)}, /*index=5*/f32[8]{0:T(128)S(1)}, f3...) while((s32[]{:T(128)}, f32[16,64]{1,0:T(8,128)S(1)}, f32[]{:T(128)}, ...), condition=%wide.region_8.9_spmd, body=%wide.region_7.8_spmd.sunk | while | flops 4110 | bytes 12555 | solution.py:35
  317.2 1.8 copy.139
  319.1 1.8 copy.136
  321.2 2.9 convolution_multiply_fusion.3
  326.1 2.8 fusion.9
  328.9 1.3 copy.143
  332.0 2.4 fusion.24
  334.4 1.8 fusion.10
  337.2 4.9 %all-gather.25.cloned.1.call-done = bf16[4,128,1024]{2,1,0:T(8,128)(2,1)} async-done(((bf16[1,128,1024]{2,1,0:T(8,128)(2,1)}), bf16[4,128,1024]{2,1,0:T(8,128)(2,1)}) %all-gather.25.cloned.1.call-update) | async-done | bytes 1048592 | tf_op jit(solution)/shard_map/all_gather | solution.py:256
  342.1 2.5 gather_fusion.7
  344.6 26.0 %all-gather.21.cloned.1.call-done = bf16[4,128,1024]{2,1,0:T(8,128)(2,1)} async-done(((bf16[1,128,1024]{2,1,0:T(8,128)(2,1)}), bf16[4,128,1024]{2,1,0:T(8,128)(2,1)}) %all-gather.21.cloned.1.call-update) | async-done | bytes 1048592 | tf_op jit(solution)/shard_map/all_gather | solution.py:254
  370.6 2.5 gather_fusion.5
  373.1 26.6 %all-gather.19.cloned.1.call-done = bf16[4,128,1024]{2,1,0:T(8,128)(2,1)} async-done(((bf16[1,128,1024]{2,1,0:T(8,128)(2,1)}), bf16[4,128,1024]{2,1,0:T(8,128)(2,1)}) %all-gather.19.cloned.1.call-update) | async-done | bytes 1048592 | tf_op jit(solution)/shard_map/all_gather | solution.py:253
  399.7 2.5 gather_fusion.4
  402.2 34.7 %all-gather.23.cloned.1.call-done = bf16[4,128,2048]{2,1,0:T(8,128)(2,1)} async-done(((bf16[1,128,2048]{2,1,0:T(8,128)(2,1)}), bf16[4,128,2048]{2,1,0:T(8,128)(2,1)}) %all-gather.23.cloned.1.call-update) | async-done | bytes 2097168 | tf_op jit(solution)/shard_map/all_gather | solution.py:255
  436.9 3.0 gather_fusion.6
  (121 shorter events, 41.6 us)
Async XLA Ops:
  7.2 38.3 %all-gather.15.cloned.1.call-start = ((), (), s32[]{:S(2)}) async-start(), calls=%async_computation.1 | async-start | bytes 1310720 | tf_op jit(solution)/shard_map/all_gather | solution.py:196
  7.9 66.1 %all-gather.17.cloned.1.call-start = ((), (), s32[]{:S(2)}) async-start(), calls=%async_computation.2 | async-start | bytes 1310720 | tf_op jit(solution)/shard_map/all_gather | solution.py:194
  8.6 102.6 %all-gather.13.cloned.1.call-start = ((), (), s32[]{:S(2)}) async-start(), calls=%async_computation | async-start | bytes 2621440 | tf_op jit(solution)/shard_map/all_gather | solution.py:195
  9.4 151.2 %all-gather.29.cloned.1.call-start = ((), (), s32[]{:S(2)}) async-start(), calls=%async_computation.8 | async-start | bytes 4718592 | tf_op jit(solution)/shard_map/all_gather | solution.py:26
  9.4 10.5 %collective-permute-start = (bf16[1,128,1024]{2,1,0:T(8,128)(2,1)}, bf16[1,128,1024]{2,1,0:T(8,128)(2,1)S(1)}, u32[]{:S(2)}, u32[]{:S(2)}) collective-permute-start(bf16[1,128,1024]{2,1,0:T(8,128)(2,1)} %param.13), channel_id=1, source_target_pairs={{0,8},{8,16},{16,24},{24,0},{1,9},{9,17},{17,25},{25,1},{2,10},{10... | collective-permute-start | bytes 786440 | tf_op jit(solution)/shard_map/ppermute | solution.py:17
  19.9 11.2 %collective-permute-start.1 = (bf16[1,128,1024]{2,1,0:T(8,128)(2,1)S(1)}, bf16[1,128,1024]{2,1,0:T(8,128)(2,1)S(1)}, u32[]{:S(2)}, u32[]{:S(2)}) collective-permute-start(bf16[1,128,1024]{2,1,0:T(8,128)(2,1)S(1)} %collective-permute-done), channel_id=1, source_target_pairs={{0,8},{8,16},{16,24},{24,0},{1,9},{9,17},{17,25},{25,1},{2,10},{10... | collective-permute-start | bytes 786440 | tf_op jit(solution)/shard_map/ppermute | solution.py:17
  31.1 12.9 %collective-permute-start.2 = (bf16[1,128,1024]{2,1,0:T(8,128)(2,1)S(1)}, bf16[1,128,1024]{2,1,0:T(8,128)(2,1)S(1)}, u32[]{:S(2)}, u32[]{:S(2)}) collective-permute-start(bf16[1,128,1024]{2,1,0:T(8,128)(2,1)S(1)} %collective-permute-done.1), channel_id=1, source_target_pairs={{0,8},{8,16},{16,24},{24,0},{1,9},{9,17},{17,25},{25,1},{2,10},{10... | collective-permute-start | bytes 786440 | tf_op jit(solution)/shard_map/ppermute | solution.py:17
  45.3 7.9 %copy-start.5 = (f32[128,16,64]{0,2,1:T(8,128)}, f32[128,16,64]{0,2,1:T(8,128)S(1)}, u32[]{:S(2)}) copy-start(f32[128,16,64]{0,2,1:T(8,128)S(1)} %copy.125) | copy-start | bytes 1572868
  50.4 0.8 copy-start
  53.2 63.1 %copy-start.8 = (u32[32]{0:T(128)S(1)}, u32[32]{0:T(128)}, u32[]{:S(2)}) copy-start(u32[32]{0:T(128)} %constant.330) | copy-start | bytes 388
  53.2 82.2 %copy-start.7 = (s32[1,128]{1,0:T(1,128)S(1)}, s32[1,128]{1,0:T(1,128)}, u32[]{:S(2)}) copy-start(s32[1,128]{1,0:T(1,128)} %param.18) | copy-start | bytes 1540
  53.2 155.2 %all-gather.27.cloned.1.call-start = ((), (), s32[]{:S(2)}) async-start(), calls=%async_computation.7 | async-start | bytes 4718592 | tf_op jit(solution)/shard_map/all_gather | solution.py:26
  115.0 227.1 %all-gather.25.cloned.1.call-start = ((), (), s32[]{:S(2)}) async-start(), calls=%async_computation.6 | async-start | bytes 1310720 | tf_op jit(solution)/shard_map/all_gather | solution.py:256
  208.7 3.1 copy-start.3
  208.7 5.3 %copy-start.1 = (f32[128,16,64]{0,2,1:T(8,128)S(1)}, f32[128,16,64]{0,2,1:T(8,128)}, u32[]{:S(2)}) copy-start(f32[128,16,64]{0,2,1:T(8,128)} %copy-done) | copy-start | bytes 1572868
  208.8 5.3 %copy-start.6 = (f32[128,16,64]{0,2,1:T(8,128)S(1)}, f32[128,16,64]{0,2,1:T(8,128)}, u32[]{:S(2)}) copy-start(f32[128,16,64]{0,2,1:T(8,128)} %copy-done.5) | copy-start | bytes 1572868
  317.2 53.4 %all-gather.21.cloned.1.call-start = ((), (), s32[]{:S(2)}) async-start(), calls=%async_computation.4 | async-start | bytes 1310720 | tf_op jit(solution)/shard_map/all_gather | solution.py:254
  319.0 80.6 %all-gather.19.cloned.1.call-start = ((), (), s32[]{:S(2)}) async-start(), calls=%async_computation.3 | async-start | bytes 1310720 | tf_op jit(solution)/shard_map/all_gather | solution.py:253
  320.9 116.0 %all-gather.23.cloned.1.call-start = ((), (), s32[]{:S(2)}) async-start(), calls=%async_computation.5 | async-start | bytes 2621440 | tf_op jit(solution)/shard_map/all_gather | solution.py:255
  324.1 1.0 copy-start.4
  326.1 8.3 %copy-start.2 = (f32[128,16,64]{0,2,1:T(8,128)S(1)}, f32[128,16,64]{0,2,1:T(8,128)}, u32[]{:S(2)}) copy-start(f32[128,16,64]{0,2,1:T(8,128)} %copy-done) | copy-start | bytes 1572868
Sparse Core Ops, SparseCore 0:
  9.8 35.6 all-gather.14
  47.3 26.6 all-gather.16
  75.9 35.2 all-gather.12
  112.7 47.8 all-gather.28
  162.6 45.8 all-gather.26
  317.3 24.7 all-gather.24
  343.9 26.6 all-gather.20
  373.0 26.6 all-gather.18
  401.5 35.2 all-gather.22
